TPU v7x, 32 devices: a whole 2x2x4 slice. The times are simulated.
32 devices in a mesh: grp: 4 (over z), mem: 8 (over y, x, core).
Axes of the slice: x: 2, y: 2, z: 4, core: 2. Of those that a mesh axis runs over, the one named last changes fastest.
Arguments:
- volume: float32 [4, 8, 8, 512, 1024], P('grp', 'mem'), may hold values from -1 to 1
- transfer_coef: float32 [4, 4], replicated, may hold values from -3 to 3
- group_order: int32 [4], replicated, may hold values from 0 to 3, each once
- member_order: int32 [4, 8], replicated, may hold values from 0 to 7, each once within a row
- active_mask: int32 [4, 8], P('grp', 'mem'), may hold values 0 or 1
Outputs:
- picture: float32 [4, 512, 1024], P(None, 'mem', 'grp')
All inputs are finite; a program needn't handle non-finite values. No bound on the sum of `active_mask` on one device may be relied on, other than what follows from the above.
Results may differ from a plain program's by a relative error of at most 0.0003.
Values sent between devices are 32-bit elements; how exact they have to be, the bound alone decides.
A program may use at most 192 MiB of HBM per device.

v0:
```python
import jax
import jax.numpy as jnp
from jax import lax
from jax.sharding import PartitionSpec as P


def polynomial(coef_row, values):
    return coef_row[0] + values * (coef_row[1] + values * (coef_row[2] + values * coef_row[3]))


def march_brick(samples, transfer_coef, active_flag, density_scale):
    optical_depth = jnp.zeros(samples.shape[1:], jnp.float32)
    colour = jnp.zeros((3,) + samples.shape[1:], jnp.float32)
    for sample_index in range(samples.shape[0]):
        values = samples[sample_index]
        extinction = polynomial(transfer_coef[3], values) ** 2 * density_scale
        opacity = 1.0 - jnp.exp(-extinction)
        tinted = jax.nn.sigmoid(
            jnp.stack([polynomial(transfer_coef[channel], values) for channel in range(3)])
        )
        colour = colour + (jnp.exp(-optical_depth) * opacity)[None] * tinted
        optical_depth = optical_depth + extinction
    coverage = 1.0 - jnp.exp(-optical_depth)
    return jnp.concatenate([colour, coverage[None]], 0) * active_flag


def reorder(layers, rank_list):
    total = rank_list.shape[0]
    positions = jnp.arange(total, dtype=jnp.int32)
    inverse = jnp.sum(
        positions[:, None] * (rank_list[:, None] == positions[None, :]).astype(jnp.int32), axis=0
    )
    return jnp.take(layers, inverse, axis=0)


def over_tree(layers):
    while layers.shape[0] > 1:
        nearer = layers[0::2]
        farther = layers[1::2]
        layers = nearer + (1.0 - nearer[:, 3:4]) * farther
    return layers[0]


def body(volume, transfer_coef, group_order, member_order, active_mask):
    groups = lax.axis_size("grp")
    members = lax.axis_size("mem")
    density_scale = 3.0 / (volume.shape[2] * groups * members)
    active_flag = active_mask[0, 0].astype(jnp.float32)
    layer = march_brick(volume[0, 0], transfer_coef, active_flag, density_scale)
    slab_ranks = lax.dynamic_slice_in_dim(member_order, lax.axis_index("grp"), 1, 0)[0]
    slab_image = over_tree(
        reorder(
            lax.all_to_all(layer[None], "mem", split_axis=2, concat_axis=0, tiled=True), slab_ranks
        )
    )
    return over_tree(
        reorder(
            lax.all_to_all(slab_image[None], "grp", split_axis=3, concat_axis=0, tiled=True),
            group_order,
        )
    )


def solution(mesh):
    in_specs = (P("grp", "mem", None, None, None), P(), P(), P(), P("grp", "mem"))
    out_specs = P(None, "mem", "grp")
    return jax.shard_map(body, mesh=mesh, in_specs=in_specs, out_specs=out_specs, check_vma=False)
```

profile of v0, /device:TPU:0, one launch (start us, length us, event | category | flops | bytes accessed | tf_op | source)
XLA Modules:
  0.0 447.8 jit_solution(17760567947958751179)
XLA Ops:
  0.0 6.7 %slice_bitcast_fusion = (f32[1,512,1024]{2,1,0:T(8,128)S(1)}, f32[1,1,1,512,1024]{4,3,2,1,0:T(8,128)S(1)}, f32[1,1,1,512,1024]{4,3,2,1,0:T(8,128)S(1)}, f32[1,1,...) fusion(f32[1,1,8,512,1024]{4,3,2,1,0:T(8,128)} %param.5), kind=kLoop, calls=%fused_computation.159 | loop fusion | bytes 33554432 | tf_op jit(solution)/shard_map/squeeze | solution.py:15
  6.7 0.9 fusion.105
  7.6 31.3 %multiply_add_fusion.4 = (f32[1,512,1024]{2,0,1:T(1,128)}, f32[1,512,1024]{2,0,1:T(1,128)}, f32[1,512,1024]{2,0,1:T(1,128)}, f32[1,512,1024]{2,0,1:T(1,128)}, f3...) fusion(f32[]{:T(128)} %bitcast.9, f32[]{:T(128)} %bitcast.8, f32[]{:T(128)} %bitcast.7, f32[]{:T(128)} %bitcast.6, ...), kind=kLoop, calls=%fused_computation.130 | loop fusion | flops 18874368 | bytes 16777264 | tf_op jit(solution)/shard_map/add | solution.py:8
  39.0 30.7 %multiply_add_fusion.10 = (f32[1,512,1024]{2,0,1:T(1,128)}, f32[1,512,1024]{2,0,1:T(1,128)}, f32[1,512,1024]{2,0,1:T(1,128)}, f32[1,512,1024]{2,0,1:T(1,128)}, f...) fusion(f32[1,1,1,512,1024]{4,3,2,1,0:T(8,128)S(1)} %get-tuple-element.16, f32[]{:T(128)} %bitcast.9, f32[]{:T(128)} %bitcast.8, ...), kind=kLoop, calls=%fused_computation.137 | loop fusion | flops 18874368 | bytes 16777264 | tf_op jit(solution)/shard_map/add | solution.py:8
  69.6 30.7 %multiply_add_fusion.16 = (f32[1,512,1024]{2,0,1:T(1,128)}, f32[1,512,1024]{2,0,1:T(1,128)}, f32[1,512,1024]{2,0,1:T(1,128)}, f32[1,512,1024]{2,0,1:T(1,128)}, f...) fusion(f32[1,1,1,512,1024]{4,3,2,1,0:T(8,128)S(1)} %get-tuple-element.18, f32[]{:T(128)} %bitcast.9, f32[]{:T(128)} %bitcast.8, ...), kind=kLoop, calls=%fused_computation.145 | loop fusion | flops 18874368 | bytes 16777264 | tf_op jit(solution)/shard_map/add | solution.py:8
  100.3 32.0 %multiply_add_fusion.22 = (f32[1,512,1024]{2,0,1:T(1,128)}, f32[1,512,1024]{2,0,1:T(1,128)}, f32[1,512,1024]{2,0,1:T(1,128)}, f32[1,512,1024]{2,0,1:T(1,128)}, f...) fusion(f32[1,1,1,512,1024]{4,3,2,1,0:T(8,128)S(1)} %get-tuple-element.20, f32[]{:T(128)} %bitcast.9, f32[]{:T(128)} %bitcast.8, ...), kind=kLoop, calls=%fused_computation.153 | loop fusion | flops 18874368 | bytes 16777264 | tf_op jit(solution)/shard_map/add | solution.py:8
  132.3 41.6 %fusion.86 = f32[1,1,512,1024]{3,1,0,2:T(1,128)} fusion(f32[1,1,1,512,1024]{4,3,2,1,0:T(8,128)S(1)} %get-tuple-element.16, f32[1,1,1,512,1024]{4,3,2,1,0:T(8,128)S(1)} %get-tuple-element.17, f32[1,1,1,512,1024]{4,3,2,1,0:T(8,128)S(1)} %get-tuple-element.18, f32[1,1,1,512,1024]{4,3,2,1,0:T(8,128)S(1)} %get-tuple-element.19, ...), kind=kLoop, calls=%fused_computation.126 | loop fusion | flops 34603008 | bytes 18874384 | tf_op jit(solution)/shard_map/concatenate | solution.py:24
  174.0 6.2 %subtract_multiply_fusion.3 = (f32[512,1024]{1,0:T(8,128)}, f32[512,1024]{1,0:T(8,128)S(1)}) fusion(f32[]{:T(128)} %bitcast.5, f32[]{:T(128)} %bitcast.4, f32[]{:T(128)} %bitcast.3, f32[]{:T(128)} %bitcast.1, f32[1,1,8,512,1024]{4,3,2,1,0:T(8,128)S(1)} %bitcast.282), kind=kLoop, calls=%fused_computation.146 | loop fusion | flops 19922944 | bytes 12582928 | tf_op jit(solution)/shard_map/mul | solution.py:21
  180.2 6.7 %subtract_multiply_fusion.1 = (f32[512,1024]{1,0:T(8,128)}, f32[512,1024]{1,0:T(8,128)S(1)}, f32[512,1024]{1,0:T(8,128)}) fusion(f32[]{:T(128)} %bitcast.5, f32[]{:T(128)} %bitcast.4, f32[]{:T(128)} %bitcast.3, f32[]{:T(128)} %bitcast.1, f32[1,1,8,512,1024]{4,3,2,1,0:T(8,128)S(1)} %bitcast.282, f32[512,1024]{1,0:T(8,128)S(1)} %get-tuple-element.6), kind=kLoop, calls=%fused_computation.138 | loop fusion | flops 17825792 | bytes 14680080 | tf_op jit(solution)/shard_map/mul | solution.py:21
  187.0 11.5 %subtract_multiply_fusion = (f32[512,1024]{1,0:T(8,128)}, f32[512,1024]{1,0:T(8,128)}, f32[512,1024]{1,0:T(8,128)}, f32[512,1024]{1,0:T(8,128)}, f32[512,1024]{1,0:T(8,128)}) fusion(f32[]{:T(128)} %bitcast.5, f32[]{:T(128)} %bitcast.4, f32[]{:T(128)} %bitcast.3, f32[]{:T(128)} %bitcast.1, f32[512,1024]{1,0:T(8,128)S(1)} %get-tuple-element.8, ...), kind=kLoop, calls=%fused_computation.134 | loop fusion | flops 35651584 | bytes 25165840 | tf_op jit(solution)/shard_map/mul | solution.py:21
  199.2 75.1 %fusion.39 = f32[1,3,512,1024]{3,1,0,2:T(4,128)S(1)} fusion(f32[1,512,1024]{2,0,1:T(1,128)S(1)} %copy-done.4, f32[1,512,1024]{2,0,1:T(1,128)S(1)} %copy-done.5, f32[1,512,1024]{2,0,1:T(1,128)S(1)} %copy-done.3, f32[1,512,1024]{2,0,1:T(1,128)S(1)} %copy-done.6, f32[1,512,1024]{2,0,1:T(1,128)S(1)} %copy-done.7, f32[1,512,1024]{2,0,1:T(1,128)S(1)} %copy-done.8, ...), kind=kLoop, calls=%fused_computation.51 | loop fusion | flops 86507520 | bytes 73400320 | tf_op jit(solution)/shard_map/concatenate | solution.py:24
  274.3 7.1 %maximum_multiply_fusion = f32[1,4,512,1024]{3,1,0,2:T(4,128)} fusion(f32[1,1,512,1024]{3,1,0,2:T(1,128)} %fusion.86, f32[1,3,512,1024]{3,1,0,2:T(4,128)S(1)} %fusion.39, f32[]{:T(128)} %bitcast.29), kind=kLoop, calls=%fused_computation.49 | loop fusion | flops 4194304 | bytes 16777220 | tf_op jit(solution)/shard_map/mul | solution.py:24
  281.4 5.2 %all-to-all-start = ((f32[1,4,512,1024]{3,1,0,2:T(4,128)}), f32[1,4,512,1024]{3,1,0,2:T(4,128)}, u32[]{:S(2)}, u32[]{:S(2)}) async-start(f32[1,4,512,1024]{3,1,0,2:T(4,128)} %maximum_multiply_fusion), calls=%async_computation | async-start | bytes 16777216 | tf_op jit(solution)/shard_map/all_to_all | solution.py:53
  286.7 94.7 %all-to-all-done = f32[1,4,512,1024]{3,1,0,2:T(4,128)} async-done(((f32[1,4,512,1024]{3,1,0,2:T(4,128)}), f32[1,4,512,1024]{3,1,0,2:T(4,128)}, u32[]{:S(2)}, u32[]{:S(2)}) %all-to-all-start) | async-done | bytes 8388640 | tf_op jit(solution)/shard_map/all_to_all | solution.py:53
  381.4 11.3 %copy.99 = f32[1,4,8,64,1024]{4,3,1,2,0:T(8,128)} copy(f32[1,4,8,64,1024]{4,1,3,2,0:T(4,128)} %bitcast.30) | data formatting | bytes 16777216 | tf_op jit(solution)/shard_map/all_to_all | solution.py:53
  392.7 7.7 %gather_fusion = f32[8,4,64,1024]{3,2,1,0:T(8,128)} fusion(f32[8,4,64,1024]{3,2,1,0:T(8,128)} %bitcast.283, s32[1024]{0:T(1024)S(1)} %pad_clamp_fusion.1), kind=kCustom, calls=%fused_computation | custom fusion | bytes 16777248 | tf_op jit(solution)/shard_map/jit(_take)/gather | solution.py:33
  400.4 4.4 broadcast_select_fusion
  404.8 0.5 slice.148
  405.5 1.1 multiply_add_fusion
  406.8 0.7 multiply_add_fusion.1
  407.5 0.2 fusion.93
  407.7 0.9 copy.75
  408.7 2.9 reshape.2041
  411.6 5.4 %all-to-all-start.1 = ((f32[4,1,65536]{2,1,0:T(1,128)}), f32[4,1,65536]{2,1,0:T(1,128)S(1)}, u32[]{:S(2)}, u32[]{:S(2)}) async-start(f32[4,1,65536]{2,1,0:T(1,128)} %reshape.2041), calls=%async_computation.1 | async-start | bytes 2097152 | tf_op jit(solution)/shard_map/all_to_all | solution.py:58
  417.1 22.5 %all-to-all-done.1 = f32[4,1,65536]{2,1,0:T(1,128)S(1)} async-done(((f32[4,1,65536]{2,1,0:T(1,128)}), f32[4,1,65536]{2,1,0:T(1,128)S(1)}, u32[]{:S(2)}, u32[]{:S(2)}) %all-to-all-start.1) | async-done | bytes 1048608 | tf_op jit(solution)/shard_map/all_to_all | solution.py:58
  439.5 0.5 broadcast.2075
  440.0 3.8 reduce
  443.8 1.4 reshape.2042
  445.2 0.8 copy.77
  446.1 0.6 gather_fusion.1
  446.7 0.2 broadcast_select_fusion.1
  447.1 0.7 fusion.97
  (48 shorter events, 0.7 us)
Async XLA Ops:
  0.0 286.6 %copy-start = (s32[4,8]{1,0:T(4,128)S(1)}, s32[4,8]{1,0:T(4,128)}, u32[]{:S(2)}) copy-start(s32[4,8]{1,0:T(4,128)} %param.8) | copy-start | bytes 388
  0.0 6.7 %copy-start.9 = (f32[4,4]{1,0:T(4,128)S(1)}, f32[4,4]{1,0:T(4,128)}, u32[]{:S(2)}) copy-start(f32[4,4]{1,0:T(4,128)} %param.6) | copy-start | bytes 196
  6.7 32.2 %copy-start.1 = (f32[1,1,1,512,1024]{4,3,2,1,0:T(8,128)}, f32[1,1,1,512,1024]{4,3,2,1,0:T(8,128)S(1)}, u32[]{:S(2)}) copy-start(f32[1,1,1,512,1024]{4,3,2,1,0:T(8,128)S(1)} %get-tuple-element.22) | copy-start | bytes 6291460
  100.3 32.0 %copy-start.2 = (f32[1,1,1,512,1024]{4,3,2,1,0:T(8,128)S(1)}, f32[1,1,1,512,1024]{4,3,2,1,0:T(8,128)}, u32[]{:S(2)}) copy-start(f32[1,1,1,512,1024]{4,3,2,1,0:T(8,128)} %copy-done.1) | copy-start | bytes 6291460
  100.3 73.6 %slice-start = ((s8[16777216]{0:T(1024)(128)(4,1)}), s8[4194304]{0:T(1024)(128)(4,1)S(1)}, s32[]{:S(2)}) async-start(s8[16777216]{0:T(1024)(128)(4,1)} %bitcast.281), calls=%async_computation.2 | async-start | bytes 8388608
  100.3 73.6 %slice-start.1 = ((s8[16777216]{0:T(1024)(128)(4,1)}), s8[4194304]{0:T(1024)(128)(4,1)S(1)}, s32[]{:S(2)}) async-start(s8[16777216]{0:T(1024)(128)(4,1)} %bitcast.281), calls=%async_computation.3 | async-start | bytes 8388608
  132.3 41.6 %slice-start.2 = ((s8[16777216]{0:T(1024)(128)(4,1)}), s8[4194304]{0:T(1024)(128)(4,1)S(1)}, s32[]{:S(2)}) async-start(s8[16777216]{0:T(1024)(128)(4,1)} %bitcast.281), calls=%async_computation.4 | async-start | bytes 8388608
  132.3 41.6 %slice-start.3 = ((s8[16777216]{0:T(1024)(128)(4,1)}), s8[4194304]{0:T(1024)(128)(4,1)S(1)}, s32[]{:S(2)}) async-start(s8[16777216]{0:T(1024)(128)(4,1)} %bitcast.281), calls=%async_computation.5 | async-start | bytes 8388608
  187.0 12.2 %copy-start.3 = (f32[1,512,1024]{2,0,1:T(1,128)S(1)}, f32[1,512,1024]{2,0,1:T(1,128)}, u32[]{:S(2)}) copy-start(f32[1,512,1024]{2,0,1:T(1,128)} %get-tuple-element.44) | copy-start | bytes 6291460
  187.0 12.2 %copy-start.4 = (f32[1,512,1024]{2,0,1:T(1,128)S(1)}, f32[1,512,1024]{2,0,1:T(1,128)}, u32[]{:S(2)}) copy-start(f32[1,512,1024]{2,0,1:T(1,128)} %get-tuple-element.45) | copy-start | bytes 6291460
  187.0 12.2 %copy-start.5 = (f32[1,512,1024]{2,0,1:T(1,128)S(1)}, f32[1,512,1024]{2,0,1:T(1,128)}, u32[]{:S(2)}) copy-start(f32[1,512,1024]{2,0,1:T(1,128)} %get-tuple-element.46) | copy-start | bytes 6291460
  187.0 12.2 %copy-start.6 = (f32[1,512,1024]{2,0,1:T(1,128)S(1)}, f32[1,512,1024]{2,0,1:T(1,128)}, u32[]{:S(2)}) copy-start(f32[1,512,1024]{2,0,1:T(1,128)} %get-tuple-element.63) | copy-start | bytes 6291460
  187.0 12.2 %copy-start.7 = (f32[1,512,1024]{2,0,1:T(1,128)S(1)}, f32[1,512,1024]{2,0,1:T(1,128)}, u32[]{:S(2)}) copy-start(f32[1,512,1024]{2,0,1:T(1,128)} %get-tuple-element.64) | copy-start | bytes 6291460
  187.0 12.2 %copy-start.8 = (f32[1,512,1024]{2,0,1:T(1,128)S(1)}, f32[1,512,1024]{2,0,1:T(1,128)}, u32[]{:S(2)}) copy-start(f32[1,512,1024]{2,0,1:T(1,128)} %get-tuple-element.65) | copy-start | bytes 6291460
  281.4 100.0 %all-to-all-start = ((f32[1,4,512,1024]{3,1,0,2:T(4,128)}), f32[1,4,512,1024]{3,1,0,2:T(4,128)}, u32[]{:S(2)}, u32[]{:S(2)}) async-start(f32[1,4,512,1024]{3,1,0,2:T(4,128)} %maximum_multiply_fusion), calls=%async_computation | async-start | bytes 16777216 | tf_op jit(solution)/shard_map/all_to_all | solution.py:53
  408.7 8.3 %copy-start.10 = (s32[4]{0:T(128)S(1)}, s32[4]{0:T(128)}, u32[]{:S(2)}) copy-start(s32[4]{0:T(128)} %param.7) | copy-start | bytes 52
  411.6 27.9 %all-to-all-start.1 = ((f32[4,1,65536]{2,1,0:T(1,128)}), f32[4,1,65536]{2,1,0:T(1,128)S(1)}, u32[]{:S(2)}, u32[]{:S(2)}) async-start(f32[4,1,65536]{2,1,0:T(1,128)} %reshape.2041), calls=%async_computation.1 | async-start | bytes 2097152 | tf_op jit(solution)/shard_map/all_to_all | solution.py:58
where the time goes:
time: 450 us; the launch traced here: 448 us
  other arithmetic  285 us (63%)
  waiting for transfers between devices  117 us (26%)
  local copies, waits for them, and re-layouts  34.6 us (8%)
  starting transfers between devices  10.6 us (2%)
    add x4, other arithmetic, polynomial(): coef_row[0]  125 us
    concatenate x2, other arithmetic, march_brick(): return jnp.concatenate([colour, coverage[None]], 0) * active_flag  117 us
    all_to_all x1, waiting for transfers between devices, body(): lax.all_to_all(layer[None], 'mem', split_axis=2, concat_axis=0, tiled=True)  94.7 us
    mul x3, other arithmetic, march_brick(): colour = colour + (jnp.exp(-optical_depth) * opacity)[None] * tinted  24.5 us
    all_to_all x1, waiting for transfers between devices, body(): lax.all_to_all(slab_image[None], 'grp', split_axis=3, concat_axis=0, tile...  22.5 us
    all_to_all x1, local copies, waits for them, and re-layouts, body(): lax.all_to_all(layer[None], 'mem', split_axis=2, concat_axis=0, tiled=True)  11.3 us
  transfers between devices with their start and end apart: 2, of which 2 were waited for; matrix products, arithmetic and copies ran while one was open for 0% of the time, Pallas kernels for 0%

commit v1 on v0

v1 whole, which is shorter than its diff:
```python
import functools
import math

import jax
import jax.numpy as jnp
from jax import lax
from jax.experimental import pallas as pl
from jax.experimental.pallas import tpu as pltpu
from jax.sharding import PartitionSpec as P

MESH = pl.DeviceIdType.MESH
CHUNKS = 4
TILE_ROWS = 8


def kernel(groups, members, coef_ref, group_ref, member_ref, active_ref, volume_ref, out_ref,
           vol, tloc, tin, col, pcol, mout, min_, tnear, tslab, sout, sin, zout, zin,
           vol_sem, t_send, t_recv, c_send, c_recv, m_send, m_recv, s_send, s_recv, z_send, z_recv):
    chunks, _, samples, rows, cols = vol.shape
    block_rows = chunks * rows
    chips = members // 2
    group_cols = cols // groups
    g = lax.axis_index("grp")
    me = lax.axis_index("mem")
    chip = me // 2
    core = me % 2
    partner = me + 1 - 2 * core
    row_tiles = rows // TILE_ROWS

    def fetch(j, d):
        start = pl.multiple_of(d * block_rows + j * rows, TILE_ROWS)
        return pltpu.make_async_copy(
            volume_ref.at[0, 0, :, pl.ds(start, rows), :], vol.at[j, d], vol_sem.at[j, d])

    def send_t(j, d, src):
        return pltpu.make_async_remote_copy(
            tloc.at[j, d], tin.at[j, src], t_send.at[j, d], t_recv.at[j, src],
            device_id={"mem": d}, device_id_type=MESH)

    def send_col(j, k):
        return pltpu.make_async_remote_copy(
            col.at[j, 2 * k + 1 - core], pcol.at[j, k], c_send.at[j, k], c_recv.at[j, k],
            device_id={"mem": partner}, device_id_type=MESH)

    def send_m(j, k, src):
        return pltpu.make_async_remote_copy(
            mout.at[j, k], min_.at[j, src], m_send.at[j, k], m_recv.at[j, src],
            device_id={"mem": 2 * k + core}, device_id_type=MESH)

    def send_s(j, k, src):
        return pltpu.make_async_remote_copy(
            sout.at[j, k], sin.at[j, src], s_send.at[j, k], s_recv.at[j, src],
            device_id={"mem": 2 * k + core}, device_id_type=MESH)

    def send_z(j, k, src):
        return pltpu.make_async_remote_copy(
            zout.at[j, k], zin.at[j, src], z_send.at[j, k], z_recv.at[j, src],
            device_id={"grp": k}, device_id_type=MESH)

    def each(count, fn):
        def step(i, carry):
            fn(i)
            return carry
        lax.fori_loop(0, count, step, 0)

    each(chunks, lambda j: each(members, lambda off: fetch(j, (me + 1 + off) % members).start()))

    barrier = pltpu.get_barrier_semaphore()
    each(members - 1, lambda off: pl.semaphore_signal(
        barrier, inc=1, device_id={"mem": (me + 1 + off) % members}, device_id_type=MESH))
    each(groups - 1, lambda off: pl.semaphore_signal(
        barrier, inc=1, device_id={"grp": (g + 1 + off) % groups}, device_id_type=MESH))
    pl.semaphore_wait(barrier, members + groups - 2)

    density_factor = math.sqrt(3.0 / (samples * groups * members) * math.log2(math.e))
    coef = [[coef_ref[c, p] * (0.5 if c < 3 else density_factor) for p in range(4)] for c in range(4)]
    active = active_ref[0, 0].astype(jnp.float32)
    half_active = active * 0.5
    width = min(256, cols)
    col_tiles = cols // width
    ranks = [member_ref[g, i] for i in range(members)]
    near = [jnp.minimum(ranks[2 * q], ranks[2 * q + 1]) for q in range(chips)]
    far = [jnp.maximum(ranks[2 * q], ranks[2 * q + 1]) for q in range(chips)]
    own_first = member_ref[g, me] < member_ref[g, partner]
    orders = [group_ref[i] for i in range(groups)]

    def tiles(fn, count=None):
        def step(i, carry):
            row = pl.ds(pl.multiple_of((i // col_tiles) * TILE_ROWS, TILE_ROWS), TILE_ROWS)
            column = pl.ds(pl.multiple_of((i % col_tiles) * width, width), width)
            fn(row, column)
            return carry
        lax.fori_loop(0, row_tiles * col_tiles, step, 0)

    def march(j, d):
        def tile(row, column):
            depth = jnp.zeros((TILE_ROWS, width), jnp.float32)
            light = jnp.ones((TILE_ROWS, width), jnp.float32)
            colour = [jnp.zeros((TILE_ROWS, width), jnp.float32) for _ in range(3)]
            for k in range(samples):
                v = vol[j, d, k, row, column]
                poly = [q[0] + v * (q[1] + v * (q[2] + v * q[3])) for q in coef]
                depth = depth - poly[3] * poly[3]
                after = jnp.exp2(depth)
                weight = light - after
                light = after
                colour = [colour[c] + weight * jnp.tanh(poly[c]) for c in range(3)]
            coverage = 1.0 - light
            tloc[j, d, row, column] = 1.0 - active * coverage
            for c in range(3):
                col[j, d, c, row, column] = half_active * (coverage + colour[c])
        tiles(tile)

    def produce(j):
        def unit(off):
            d = (me + 1 + off) % members
            fetch(j, d).wait()
            march(j, d)

            @pl.when(off < members - 1)
            def _():
                send_t(j, d, me).start()

            @pl.when(d % 2 != core)
            def _():
                send_col(j, d // 2).start()
        each(members, unit)

        def keep(row, column):
            tin[j, me, row, column] = tloc[j, me, row, column]
        tiles(keep)

    def ratios(j):
        def arrive(off):
            i = (me + 1 + off) % members
            send_t(j, i, i).wait_recv()
        each(members - 1, arrive)

        def tile(row, column):
            t = [tin[j, i, row, column] for i in range(members)]
            total = t[0]
            for i in range(1, members):
                total = total * t[i]
            tslab[j, row, column] = total
            for q in range(chips):
                before = jnp.ones((TILE_ROWS, width), jnp.float32)
                between = jnp.ones((TILE_ROWS, width), jnp.float32)
                for i in range(members):
                    nearer = ranks[i] < near[q]
                    inside = jnp.logical_and(ranks[i] >= near[q], ranks[i] < far[q])
                    before = before * jnp.where(nearer, t[i], 1.0)
                    between = between * jnp.where(inside, t[i], 1.0)
                tnear[j, q, row, column] = before
                mout[j, q, row, column] = between
        tiles(tile)
        each(chips - 1, lambda off: send_m(j, (chip + 1 + off) % chips, chip).start())

        def keep(row, column):
            min_[j, chip, row, column] = mout[j, chip, row, column]
        tiles(keep)

    def pair_sums(j):
        def unit(off):
            k = (chip + 1 + off) % chips

            @pl.when(off < chips - 1)
            def _():
                send_m(j, k, k).wait_recv()
            send_col(j, k).wait_recv()

            def tile(row, column):
                ratio = min_[j, k, row, column]
                own_factor = jnp.where(own_first, 1.0, ratio)
                other_factor = jnp.where(own_first, ratio, 1.0)
                for c in range(3):
                    sout[j, k, c, row, column] = (
                        col[j, 2 * k + core, c, row, column] * own_factor
                        + pcol[j, k, c, row, column] * other_factor)
            tiles(tile)

            @pl.when(off < chips - 1)
            def _():
                send_s(j, k, chip).start()
        each(chips, unit)

        def keep(row, column):
            for c in range(3):
                sin[j, chip, c, row, column] = sout[j, chip, c, row, column]
        tiles(keep)

    def slab(j):
        def arrive(off):
            q = (chip + 1 + off) % chips
            send_s(j, q, q).wait_recv()
        each(chips - 1, arrive)

        def part(k):
            def tile(i):
                row = pl.ds(pl.multiple_of(i * TILE_ROWS, TILE_ROWS), TILE_ROWS)
                column = pl.ds(pl.multiple_of(k * group_cols, group_cols), group_cols)
                factor = [tnear[j, q, row, column] for q in range(chips)]
                for c in range(3):
                    total = factor[0] * sin[j, 0, c, row, column]
                    for q in range(1, chips):
                        total = total + factor[q] * sin[j, q, c, row, column]
                    zout[j, k, c, row, :] = total
                zout[j, k, 3, row, :] = tslab[j, row, column]
            each(row_tiles, tile)

        def unit(off):
            k = (g + 1 + off) % groups
            part(k)

            @pl.when(off < groups - 1)
            def _():
                send_z(j, k, g).start()
        each(groups, unit)
        zin[j, g] = zout[j, g]

    def finish(j):
        def arrive(off):
            i = (g + 1 + off) % groups
            send_z(j, i, i).wait_recv()
        each(groups - 1, arrive)
        for r in range(row_tiles):
            row = pl.ds(r * TILE_ROWS, TILE_ROWS)
            out_row = pl.ds(pl.multiple_of(j * rows + r * TILE_ROWS, TILE_ROWS), TILE_ROWS)
            t = [zin[j, i, 3, row, :] for i in range(groups)]
            total = t[0]
            for i in range(1, groups):
                total = total * t[i]
            out_ref[3, out_row, :] = 1.0 - total
            factor = []
            for i in range(groups):
                before = jnp.ones_like(total)
                for o in range(groups):
                    if o != i:
                        before = before * jnp.where(orders[o] < orders[i], t[o], 1.0)
                factor.append(before)
            for c in range(3):
                colour = factor[0] * zin[j, 0, c, row, :]
                for i in range(1, groups):
                    colour = colour + factor[i] * zin[j, i, c, row, :]
                out_ref[c, out_row, :] = colour

    def step(s):
        for lag, stage in enumerate((produce, ratios, pair_sums, slab, finish)):
            @pl.when(jnp.logical_and(s >= lag, s < chunks + lag))
            def _():
                stage(s - lag)
    each(chunks + 4, step)

    def drain(j):
        each(members - 1, lambda off: send_t(j, (me + 1 + off) % members, me).wait_send())
        each(chips, lambda k: send_col(j, k).wait_send())
        each(chips - 1, lambda off: send_m(j, (chip + 1 + off) % chips, chip).wait_send())
        each(chips - 1, lambda off: send_s(j, (chip + 1 + off) % chips, chip).wait_send())
        each(groups - 1, lambda off: send_z(j, (g + 1 + off) % groups, g).wait_send())
    each(chunks, drain)


def solution(mesh):
    groups, members = mesh.shape["grp"], mesh.shape["mem"]
    chips = members // 2

    def body(volume, transfer_coef, group_order, member_order, active_mask):
        samples, image_rows, cols = volume.shape[2:]
        block_rows = image_rows // members
        chunks = min(CHUNKS, block_rows // TILE_ROWS)
        rows = block_rows // chunks
        group_cols = cols // groups
        smem = pl.BlockSpec(memory_space=pltpu.SMEM)
        f32 = jnp.float32
        dma = pltpu.SemaphoreType.DMA
        scratch = [
            pltpu.VMEM((chunks, members, samples, rows, cols), f32),
            pltpu.VMEM((chunks, members, rows, cols), f32),
            pltpu.VMEM((chunks, members, rows, cols), f32),
            pltpu.VMEM((chunks, members, 3, rows, cols), f32),
            pltpu.VMEM((chunks, chips, 3, rows, cols), f32),
            pltpu.VMEM((chunks, chips, rows, cols), f32),
            pltpu.VMEM((chunks, chips, rows, cols), f32),
            pltpu.VMEM((chunks, chips, rows, cols), f32),
            pltpu.VMEM((chunks, rows, cols), f32),
            pltpu.VMEM((chunks, chips, 3, rows, cols), f32),
            pltpu.VMEM((chunks, chips, 3, rows, cols), f32),
            pltpu.VMEM((chunks, groups, 4, rows, group_cols), f32),
            pltpu.VMEM((chunks, groups, 4, rows, group_cols), f32),
            dma((chunks, members)),
            dma((chunks, members)), dma((chunks, members)),
            dma((chunks, chips)), dma((chunks, chips)),
            dma((chunks, chips)), dma((chunks, chips)),
            dma((chunks, chips)), dma((chunks, chips)),
            dma((chunks, groups)), dma((chunks, groups)),
        ]
        return pl.pallas_call(
            functools.partial(kernel, groups, members),
            out_shape=jax.ShapeDtypeStruct((4, block_rows, group_cols), f32),
            in_specs=[smem, smem, smem, smem, pl.BlockSpec(memory_space=pl.ANY)],
            out_specs=pl.BlockSpec(memory_space=pltpu.VMEM),
            scratch_shapes=scratch,
            compiler_params=pltpu.CompilerParams(
                collective_id=0, has_side_effects=True, vmem_limit_bytes=60 * 1024 * 1024),
        )(transfer_coef, group_order, member_order, active_mask, volume)

    in_specs = (P("grp", "mem", None, None, None), P(), P(), P(), P("grp", "mem"))
    out_specs = P(None, "mem", "grp")
    return jax.shard_map(body, mesh=mesh, in_specs=in_specs, out_specs=out_specs, check_vma=False)
```

time: 450 us -> 92.6 us (0.21)
  other arithmetic: 285 us -> 0 us
  waiting for transfers between devices: 117 us -> 0 us
  Pallas kernels: 0 us -> 90.1 us
  local copies, waits for them, and re-layouts: 34.6 us -> 1.67 us
  starting transfers between devices: 10.6 us -> 0 us
    add x8 -> x0, other arithmetic: 127 us -> none  [the longest x4 125 us: polynomial(): coef_row[0]]
    all_to_all x2 -> x0, waiting for transfers between devices: 117 us -> none  [the longest x1 94.7 us: body(): lax.all_to_all(layer[None], 'mem', split_axis=2, concat_axis=0, tiled=True)]
    concatenate x2 -> x0, other arithmetic: 117 us -> none  [march_brick(): return jnp.concatenate([colour, coverage[None]], 0) * active_flag]
    pallas_call x0 -> x1, Pallas kernels: none -> 90.1 us  [body(): pl.pallas_call(functools.partial(kernel, groups, members), out_shape=jax....]
    mul x9 -> x0, other arithmetic: 31.8 us -> none  [the longest x3 24.5 us: march_brick(): colour = colour + (jnp.exp(-optical_depth) * opacity)[None] * tinted]
    all_to_all x3 -> x0, local copies, waits for them, and re-layouts: 12.7 us -> none  [the longest x1 11.3 us: body(): lax.all_to_all(layer[None], 'mem', split_axis=2, concat_axis=0, tiled=True)]
    all_to_all x2 -> x0, starting transfers between devices: 10.6 us -> none  [the longest x1 5.36 us: body(): lax.all_to_all(slab_image[None], 'grp', split_axis=3, concat_axis=0, tile...]
    gather x2 -> x0, local copies, waits for them, and re-layouts: 8.33 us -> none  [reorder(): return jnp.take(layers, inverse, axis=0)]
  transfers between devices with their start and end apart: 2 -> 0, of which waited for: 2 -> 0; matrix products, arithmetic and copies ran while one was open for 0% -> 0% of each run, Pallas kernels for 0% -> 0%
where the time goes in v1:
time: 92.6 us; the launch traced here: 92.4 us
  Pallas kernels  90.1 us (97%)
  local copies, waits for them, and re-layouts  1.67 us (2%)
    pallas_call x1, Pallas kernels, body(): pl.pallas_call(functools.partial(kernel, groups, members), out_shape=jax....  90.1 us

profile of v1, /device:TPU:0, one launch (start us, length us, event | category | flops | bytes accessed | tf_op | source)
XLA Modules:
  0.0 92.4 jit_solution(1154833880510600396)
XLA Ops:
  0.7 90.1 %shard_map.55 = f32[4,64,256]{2,1,0:T(8,128)} custom-call(f32[4,4]{1,0:T(4,128)} %coef_ref.1, s32[4]{0:T(128)} %group_ref.1, s32[4,8]{1,0:T(4,128)} %member_ref.1, s32[1,1]{1,0:T(1,128)S(6)} %copy.7.active_ref, f32[1,1,8,512,1024]{4,3,2,1,0:T(8,128)} %volume_ref.1), custom_call_target="tpu_custom_call" | custom-call | tf_op jit(solution)/shard_map/pallas_call | solution.py:296
  90.7 1.7 %copy.8 = f32[4,64,256]{2,1,0:T(8,128)} copy(f32[4,64,256]{2,1,0:T(8,128)} %shard_map.55) | data formatting | bytes 524288

commit v2 on v1

--- a/solution.py
+++ b/solution.py
@@ -10,6 +10,7 @@
 
 MESH = pl.DeviceIdType.MESH
 CHUNKS = 4
+EARLY = 3
 TILE_ROWS = 8
 
 
@@ -30,32 +31,35 @@
     def fetch(j, d):
         start = pl.multiple_of(d * block_rows + j * rows, TILE_ROWS)
         return pltpu.make_async_copy(
-            volume_ref.at[0, 0, :, pl.ds(start, rows), :], vol.at[j, d], vol_sem.at[j, d])
+            volume_ref.at[0, 0, :, pl.ds(start, rows), :], vol.at[j, d], vol_sem.at[j])
 
     def send_t(j, d, src):
         return pltpu.make_async_remote_copy(
-            tloc.at[j, d], tin.at[j, src], t_send.at[j, d], t_recv.at[j, src],
+            tloc.at[j, d], tin.at[j, src], t_send, t_recv.at[j],
             device_id={"mem": d}, device_id_type=MESH)
 
     def send_col(j, k):
         return pltpu.make_async_remote_copy(
-            col.at[j, 2 * k + 1 - core], pcol.at[j, k], c_send.at[j, k], c_recv.at[j, k],
+            col.at[j, 2 * k + 1 - core], pcol.at[j, k], c_send, c_recv.at[j],
             device_id={"mem": partner}, device_id_type=MESH)
 
     def send_m(j, k, src):
         return pltpu.make_async_remote_copy(
-            mout.at[j, k], min_.at[j, src], m_send.at[j, k], m_recv.at[j, src],
+            mout.at[j, k], min_.at[j, src], m_send, m_recv.at[j],
             device_id={"mem": 2 * k + core}, device_id_type=MESH)
 
     def send_s(j, k, src):
         return pltpu.make_async_remote_copy(
-            sout.at[j, k], sin.at[j, src], s_send.at[j, k], s_recv.at[j, src],
+            sout.at[j, k], sin.at[j, src], s_send, s_recv.at[j],
             device_id={"mem": 2 * k + core}, device_id_type=MESH)
 
     def send_z(j, k, src):
         return pltpu.make_async_remote_copy(
-            zout.at[j, k], zin.at[j, src], z_send.at[j, k], z_recv.at[j, src],
+            zout.at[j, k], zin.at[j, src], z_send, z_recv.at[j],
             device_id={"grp": k}, device_id_type=MESH)
+
+    def landed(ref, sem):
+        pltpu.make_async_copy(ref, ref, sem).wait()
 
     def each(count, fn):
         def step(i, carry):
@@ -70,13 +74,12 @@
         barrier, inc=1, device_id={"mem": (me + 1 + off) % members}, device_id_type=MESH))
     each(groups - 1, lambda off: pl.semaphore_signal(
         barrier, inc=1, device_id={"grp": (g + 1 + off) % groups}, device_id_type=MESH))
-    pl.semaphore_wait(barrier, members + groups - 2)
 
     density_factor = math.sqrt(3.0 / (samples * groups * members) * math.log2(math.e))
     coef = [[coef_ref[c, p] * (0.5 if c < 3 else density_factor) for p in range(4)] for c in range(4)]
     active = active_ref[0, 0].astype(jnp.float32)
     half_active = active * 0.5
-    width = min(256, cols)
+    width = min(512, cols)
     col_tiles = cols // width
     ranks = [member_ref[g, i] for i in range(members)]
     near = [jnp.minimum(ranks[2 * q], ranks[2 * q + 1]) for q in range(chips)]
@@ -111,11 +114,19 @@
                 col[j, d, c, row, column] = half_active * (coverage + colour[c])
         tiles(tile)
 
+    early = min(EARLY, members - 1)
+
     def produce(j):
+        @pl.when(j > 0)
+        def _():
+            landed(vol.at[j], vol_sem.at[j])
+
         def unit(off):
             d = (me + 1 + off) % members
-            fetch(j, d).wait()
-            march(j, d)
+
+            @pl.when(jnp.logical_or(j > 0, off >= early))
+            def _():
+                march(j, d)
 
             @pl.when(off < members - 1)
             def _():
@@ -131,10 +142,7 @@
         tiles(keep)
 
     def ratios(j):
-        def arrive(off):
-            i = (me + 1 + off) % members
-            send_t(j, i, i).wait_recv()
-        each(members - 1, arrive)
+        landed(tin.at[j, pl.ds(0, members - 1)], t_recv.at[j])
 
         def tile(row, column):
             t = [tin[j, i, row, column] for i in range(members)]
@@ -160,13 +168,11 @@
         tiles(keep)
 
     def pair_sums(j):
+        landed(min_.at[j, pl.ds(0, chips - 1)], m_recv.at[j])
+        landed(pcol.at[j], c_recv.at[j])
+
         def unit(off):
             k = (chip + 1 + off) % chips
-
-            @pl.when(off < chips - 1)
-            def _():
-                send_m(j, k, k).wait_recv()
-            send_col(j, k).wait_recv()
 
             def tile(row, column):
                 ratio = min_[j, k, row, column]
@@ -189,10 +195,7 @@
         tiles(keep)
 
     def slab(j):
-        def arrive(off):
-            q = (chip + 1 + off) % chips
-            send_s(j, q, q).wait_recv()
-        each(chips - 1, arrive)
+        landed(sin.at[j, pl.ds(0, chips - 1)], s_recv.at[j])
 
         def part(k):
             def tile(i):
@@ -218,10 +221,7 @@
         zin[j, g] = zout[j, g]
 
     def finish(j):
-        def arrive(off):
-            i = (g + 1 + off) % groups
-            send_z(j, i, i).wait_recv()
-        each(groups - 1, arrive)
+        landed(zin.at[j, pl.ds(0, groups - 1)], z_recv.at[j])
         for r in range(row_tiles):
             row = pl.ds(r * TILE_ROWS, TILE_ROWS)
             out_row = pl.ds(pl.multiple_of(j * rows + r * TILE_ROWS, TILE_ROWS), TILE_ROWS)
@@ -248,15 +248,16 @@
             @pl.when(jnp.logical_and(s >= lag, s < chunks + lag))
             def _():
                 stage(s - lag)
+    landed(vol.at[0], vol_sem.at[0])
+    each(early, lambda off: march(0, (me + 1 + off) % members))
+    pl.semaphore_wait(barrier, members + groups - 2)
     each(chunks + 4, step)
 
-    def drain(j):
-        each(members - 1, lambda off: send_t(j, (me + 1 + off) % members, me).wait_send())
-        each(chips, lambda k: send_col(j, k).wait_send())
-        each(chips - 1, lambda off: send_m(j, (chip + 1 + off) % chips, chip).wait_send())
-        each(chips - 1, lambda off: send_s(j, (chip + 1 + off) % chips, chip).wait_send())
-        each(groups - 1, lambda off: send_z(j, (g + 1 + off) % groups, g).wait_send())
-    each(chunks, drain)
+    landed(tloc.at[:, pl.ds(0, members - 1)], t_send)
+    landed(pcol, c_send)
+    landed(mout.at[:, pl.ds(0, chips - 1)], m_send)
+    landed(sout.at[:, pl.ds(0, chips - 1)], s_send)
+    landed(zout.at[:, pl.ds(0, groups - 1)], z_send)
 
 
 def solution(mesh):
@@ -286,12 +287,12 @@
             pltpu.VMEM((chunks, chips, 3, rows, cols), f32),
             pltpu.VMEM((chunks, groups, 4, rows, group_cols), f32),
             pltpu.VMEM((chunks, groups, 4, rows, group_cols), f32),
-            dma((chunks, members)),
-            dma((chunks, members)), dma((chunks, members)),
-            dma((chunks, chips)), dma((chunks, chips)),
-            dma((chunks, chips)), dma((chunks, chips)),
-            dma((chunks, chips)), dma((chunks, chips)),
-            dma((chunks, groups)), dma((chunks, groups)),
+            dma((chunks,)),
+            dma, dma((chunks,)),
+            dma, dma((chunks,)),
+            dma, dma((chunks,)),
+            dma, dma((chunks,)),
+            dma, dma((chunks,)),
         ]
         return pl.pallas_call(
             functools.partial(kernel, groups, members),

time: 92.6 us -> 87.9 us (0.949)
  Pallas kernels: 90.1 us -> 85.4 us
    pallas_call x1, Pallas kernels: 90.1 us -> 85.4 us  [body(): pl.pallas_call(functools.partial(kernel, groups, members), out_shape=jax....]
where the time goes in v2:
time: 87.9 us; the launch traced here: 87.7 us
  Pallas kernels  85.4 us (97%)
  local copies, waits for them, and re-layouts  1.67 us (2%)
    pallas_call x1, Pallas kernels, body(): pl.pallas_call(functools.partial(kernel, groups, members), out_shape=jax....  85.4 us

profile of v2, /device:TPU:0, one launch (start us, length us, event | category | flops | bytes accessed | tf_op | source)
XLA Modules:
  0.0 87.7 jit_solution(10195942543461176649)
XLA Ops:
  0.7 85.4 %shard_map.55 = f32[4,64,256]{2,1,0:T(8,128)} custom-call(f32[4,4]{1,0:T(4,128)} %coef_ref.1, s32[4]{0:T(128)} %group_ref.1, s32[4,8]{1,0:T(4,128)} %member_ref.1, s32[1,1]{1,0:T(1,128)S(6)} %copy.7.active_ref, f32[1,1,8,512,1024]{4,3,2,1,0:T(8,128)} %volume_ref.1), custom_call_target="tpu_custom_call" | custom-call | tf_op jit(solution)/shard_map/pallas_call | solution.py:297
  86.0 1.7 %copy.8 = f32[4,64,256]{2,1,0:T(8,128)} copy(f32[4,64,256]{2,1,0:T(8,128)} %shard_map.55) | data formatting | bytes 524288

commit v3 on v2

--- a/solution.py
+++ b/solution.py
@@ -9,8 +9,8 @@
 from jax.sharding import PartitionSpec as P
 
 MESH = pl.DeviceIdType.MESH
-CHUNKS = 4
-EARLY = 3
+CHUNKS = 8
+EARLY = 6
 TILE_ROWS = 8
 
 

time: 87.9 us -> 86.3 us (0.982)
  Pallas kernels: 85.4 us -> 83.8 us
    pallas_call x1, Pallas kernels: 85.4 us -> 83.8 us  [body(): pl.pallas_call(functools.partial(kernel, groups, members), out_shape=jax....]
where the time goes in v3:
time: 86.3 us; the launch traced here: 86.1 us
  Pallas kernels  83.8 us (97%)
  local copies, waits for them, and re-layouts  1.67 us (2%)
    pallas_call x1, Pallas kernels, body(): pl.pallas_call(functools.partial(kernel, groups, members), out_shape=jax....  83.8 us

profile of v3, /device:TPU:0, one launch (start us, length us, event | category | flops | bytes accessed | tf_op | source)
XLA Modules:
  0.0 86.1 jit_solution(14012022304509471184)
XLA Ops:
  0.7 83.8 %shard_map.55 = f32[4,64,256]{2,1,0:T(8,128)} custom-call(f32[4,4]{1,0:T(4,128)} %coef_ref.1, s32[4]{0:T(128)} %group_ref.1, s32[4,8]{1,0:T(4,128)} %member_ref.1, s32[1,1]{1,0:T(1,128)S(6)} %copy.7.active_ref, f32[1,1,8,512,1024]{4,3,2,1,0:T(8,128)} %volume_ref.1), custom_call_target="tpu_custom_call" | custom-call | tf_op jit(solution)/shard_map/pallas_call | solution.py:297
  84.4 1.7 %copy.8 = f32[4,64,256]{2,1,0:T(8,128)} copy(f32[4,64,256]{2,1,0:T(8,128)} %shard_map.55) | data formatting | bytes 524288
